TPU v7x, 32 devices: a whole 2x2x4 slice. The times are simulated.
32 devices in a mesh: seq: 8 (over z, x), tp: 4 (over y, core).
Axes of the slice: x: 2, y: 2, z: 4, core: 2. Of those that a mesh axis runs over, the one named last changes fastest.
Arguments:
- tokens: bfloat16 [2048, 1536], P('seq'), may hold values from -6 to 6
- norm1_gain: bfloat16 [1536], replicated, may hold values from 0.25 to 1.75
- w_query: bfloat16 [1536, 1536], P('tp'), may hold values from -0.15625 to 0.15625
- key_weight: bfloat16 [512, 1536], P('tp'), may hold values from -0.4375 to 0.4375
- value_weight: bfloat16 [512, 1536], P('tp'), may hold values from -0.15625 to 0.15625
- rotated_key_cache: bfloat16 [4, 8, 524288], P(None, 'tp', 'seq'), may hold values from -60 to 60
- stored_value_cache: bfloat16 [4, 8, 524288], P(None, 'tp', 'seq'), may hold values from -6 to 6
- cache_len: int32 [4], replicated, may hold values from 1 to 8192, 16384 in all
- w_out: bfloat16 [1536, 1536], P('tp'), may hold values from -0.15625 to 0.15625
- norm2_gain: bfloat16 [1536], replicated, may hold values from 0.25 to 1.75
- w_router: bfloat16 [1536, 40], replicated, may hold values from -0.0546875 to 0.0546875
- expert_ids: int32 [2048, 8], P('seq'), may hold values from 0 to 39, all different within a row
- w_gate_up: bfloat16 [40, 2, 1536, 512], P('tp', None, 'seq'), may hold values from -0.15625 to 0.15625
- w_down: bfloat16 [40, 512, 1536], P('tp', 'seq'), may hold values from -0.5 to 0.5
Outputs:
- attn_out: bfloat16 [2048, 1536], P('seq')
- expert_out: bfloat16 [2048, 1536], P('seq')
Inputs may be any that keep to these rules, and one draw needn't show every extreme that they name: `cache_len`: request lengths of 1 to 8192; one request fills all 8192 positions. `expert_ids`: each row names 8 different experts; every expert is named.
All inputs are finite; a program needn't handle non-finite values.
Results may differ from a plain program's by a relative error of at most 0.03.
Values may be sent and summed in bfloat16 or wider, within the bound.
A program may use at most 192 MiB of HBM per device.

v0:
```python
import jax
import jax.numpy as jnp
from jax import lax
from jax.sharding import PartitionSpec as P

HEAD_SIZE = 64
FRESH_TOKENS = 512
EPS = 1e-05
THETA = 10000.0
NEGATIVE = -1e30


def combined_all(x, axis, join):
    gathered = jax.tree.map(
        lambda a, kind: lax.all_gather(a.astype(kind), axis),
        x,
        (jnp.bfloat16, jnp.bfloat16, jnp.bfloat16),
    )

    def take(source):
        return jax.tree.map(
            lambda a, own: lax.dynamic_index_in_dim(a, source, 0, False).astype(own.dtype),
            gathered,
            x,
        )

    return lax.fori_loop(
        1, lax.axis_size(axis), lambda source, state: join(state, take(source)), take(0)
    )


def rms_norm(values, gain):
    mean_square = jnp.mean(values * values, axis=-1, keepdims=True)
    return values * lax.rsqrt(mean_square + EPS) * gain.astype(values.dtype)


def apply_rotary(values, positions):
    half_dim = values.shape[-1] // 2
    exponent = jnp.arange(half_dim, dtype=jnp.float32) * (2.0 / values.shape[-1])
    freqs = THETA ** (-exponent)
    angles = positions[:, None] * freqs[None, :]
    cosine = jnp.cos(angles)[:, None, :]
    sine = jnp.sin(angles)[:, None, :]
    first = values[..., :half_dim]
    second = values[..., half_dim:]
    return jnp.concatenate(
        [first * cosine - second * sine, second * cosine + first * sine], axis=-1
    )


def apply_projection(normalized_input, weight):
    return jnp.einsum("td,fd->tf", normalized_input, weight, preferred_element_type=jnp.float32)


def lookup(table, index):
    hits = index[:, None] == jnp.arange(table.shape[0], dtype=jnp.int32)[None, :]
    return jnp.sum(jnp.where(hits, table[None, :], 0), axis=1)


def join_parts(first, second):
    out_a, peak_a, sum_a = first
    out_b, peak_b, sum_b = second
    top = jnp.maximum(peak_a, peak_b)
    factor_a = jnp.exp(peak_a - top)
    factor_b = jnp.exp(peak_b - top)
    return (
        out_a * factor_a[..., None] + out_b * factor_b[..., None],
        top,
        sum_a * factor_a + sum_b * factor_b,
    )


def per_device(
    tokens,
    norm1_gain,
    w_query,
    key_weight,
    value_weight,
    rotated_key_cache,
    stored_value_cache,
    cache_len,
    w_out,
    norm2_gain,
    w_router,
    expert_ids,
    w_gate_up,
    w_down,
):
    tok_rows, width = tokens.shape
    seq_pos = lax.axis_index("seq")
    tp_pos = lax.axis_index("tp")
    local_q = w_query.shape[0] // HEAD_SIZE
    local_kv = key_weight.shape[0] // HEAD_SIZE
    query_group = local_q // local_kv
    requests = rotated_key_cache.shape[0]
    span = rotated_key_cache.shape[2] // HEAD_SIZE
    scale = HEAD_SIZE ** (-0.5)
    inputs = tokens.astype(jnp.float32)
    normalized_input = rms_norm(inputs, norm1_gain).astype(jnp.bfloat16)
    row_ids = seq_pos * tok_rows + jnp.arange(tok_rows, dtype=jnp.int32)
    owners = row_ids // FRESH_TOKENS
    positions = lookup(cache_len, owners) + row_ids % FRESH_TOKENS
    angle_position = positions.astype(jnp.float32)
    query_vector = apply_rotary(
        apply_projection(normalized_input, w_query).reshape(tok_rows, local_q, HEAD_SIZE),
        angle_position,
    ).astype(jnp.bfloat16)
    fresh_key = apply_rotary(
        apply_projection(normalized_input, key_weight).reshape(tok_rows, local_kv, HEAD_SIZE),
        angle_position,
    ).astype(jnp.bfloat16)
    fresh_value = (
        apply_projection(normalized_input, value_weight)
        .astype(jnp.bfloat16)
        .reshape(tok_rows, local_kv, HEAD_SIZE)
    )
    all_query = lax.all_gather(
        query_vector.reshape(tok_rows, local_q * HEAD_SIZE), "seq", axis=0, tiled=True
    )
    cache_pos = seq_pos * span + jnp.arange(span, dtype=jnp.int32)
    key_pos = jnp.concatenate([cache_pos, positions])

    def one_request(request_index):
        length = lax.dynamic_index_in_dim(cache_len, request_index, 0, keepdims=False)
        query_rows = lax.dynamic_slice_in_dim(
            all_query, request_index * FRESH_TOKENS, FRESH_TOKENS, 0
        ).reshape(FRESH_TOKENS, local_kv, query_group, HEAD_SIZE)
        query_pos = length + jnp.arange(FRESH_TOKENS, dtype=jnp.int32)
        prior_keys = jnp.transpose(
            lax.dynamic_index_in_dim(rotated_key_cache, request_index, 0, keepdims=False).reshape(
                local_kv, span, HEAD_SIZE
            ),
            (1, 0, 2),
        )
        prior_values = jnp.transpose(
            lax.dynamic_index_in_dim(stored_value_cache, request_index, 0, keepdims=False).reshape(
                local_kv, span, HEAD_SIZE
            ),
            (1, 0, 2),
        )
        keys = jnp.concatenate([prior_keys, fresh_key], axis=0)
        values = jnp.concatenate([prior_values, fresh_value], axis=0)
        usable = jnp.concatenate([cache_pos < length, owners == request_index])
        allowed = usable[None, :] & (key_pos[None, :] <= query_pos[:, None])
        scores = (
            jnp.einsum("nhgd,khd->hgnk", query_rows, keys, preferred_element_type=jnp.float32)
            * scale
        )
        scores = jnp.where(allowed[None, None], scores, NEGATIVE)
        peak = jnp.max(scores, axis=-1)
        weights = jnp.where(allowed[None, None], jnp.exp(scores - peak[..., None]), 0.0)
        total = jnp.sum(weights, axis=-1)
        mixed = jnp.einsum(
            "hgnk,khd->nhgd",
            weights.astype(jnp.bfloat16),
            values,
            preferred_element_type=jnp.float32,
        )
        return (
            mixed.reshape(FRESH_TOKENS, local_q, HEAD_SIZE),
            jnp.transpose(peak, (2, 0, 1)).reshape(FRESH_TOKENS, local_q),
            jnp.transpose(total, (2, 0, 1)).reshape(FRESH_TOKENS, local_q),
        )

    part_out, part_peak, part_sum = lax.map(one_request, jnp.arange(requests, dtype=jnp.int32))
    total_rows = requests * FRESH_TOKENS
    part_out = part_out.reshape(total_rows, local_q, HEAD_SIZE)
    part_peak = part_peak.reshape(total_rows, local_q)
    part_sum = part_sum.reshape(total_rows, local_q)
    full_out, full_peak, full_sum = combined_all((part_out, part_peak, part_sum), "seq", join_parts)
    own_out = lax.dynamic_slice_in_dim(full_out, seq_pos * tok_rows, tok_rows, 0)
    own_sum = lax.dynamic_slice_in_dim(full_sum, seq_pos * tok_rows, tok_rows, 0)
    heads_out = (
        (own_out / own_sum[..., None]).astype(jnp.bfloat16).reshape(tok_rows, local_q * HEAD_SIZE)
    )
    attn_part = jnp.dot(heads_out, w_out, preferred_element_type=jnp.float32)
    attn = lax.psum(attn_part.astype(jnp.bfloat16), "tp").astype(jnp.float32)
    attn_out = attn.astype(jnp.bfloat16)
    normed2 = rms_norm(inputs + attn, norm2_gain).astype(jnp.bfloat16)
    logits = jnp.dot(normed2, w_router, preferred_element_type=jnp.float32)
    experts_all = w_router.shape[1]
    picked_all = expert_ids[:, :, None] == jnp.arange(experts_all, dtype=jnp.int32)[None, None, :]
    chosen = jnp.sum(jnp.where(picked_all, logits[:, None, :], 0.0), axis=-1)
    gates = jax.nn.softmax(chosen, axis=-1)
    local_experts = w_gate_up.shape[0]
    local_ids = tp_pos * local_experts + jnp.arange(local_experts, dtype=jnp.int32)
    picked = expert_ids[:, :, None] == local_ids[None, None, :]
    share = jnp.sum(jnp.where(picked, gates[:, :, None], 0.0), axis=1)
    both = jnp.einsum(
        "td,ecdf->tecf",
        normed2,
        lax.all_gather(w_gate_up, "seq", axis=2, tiled=True),
        preferred_element_type=jnp.float32,
    )
    hidden = (jax.nn.silu(both[:, :, 0]) * both[:, :, 1] * share[:, :, None]).astype(jnp.bfloat16)
    moe_part = jnp.einsum(
        "tef,efd->td",
        hidden,
        lax.all_gather(w_down, "seq", axis=1, tiled=True),
        preferred_element_type=jnp.float32,
    )
    expert_out = lax.psum(moe_part.astype(jnp.bfloat16), "tp")
    return (attn_out, expert_out)


def solution(mesh):
    return jax.shard_map(
        per_device,
        mesh=mesh,
        in_specs=(
            P("seq", None),
            P(),
            P("tp", None),
            P("tp", None),
            P("tp", None),
            P(None, "tp", "seq"),
            P(None, "tp", "seq"),
            P(),
            P("tp", None),
            P(),
            P(),
            P("seq", None),
            P("tp", None, "seq", None),
            P("tp", "seq", None),
        ),
        out_specs=(P("seq", None), P("seq", None)),
        check_vma=False,
    )
```

profile of v0, /device:TPU:0, one launch (start us, length us, event | category | flops | bytes accessed | tf_op | source)
XLA Modules:
  0.0 1429.9 jit_solution(5135392663269853709)
XLA Ops:
  15.7 45.8 %all-gather.5.cloned.1.call-done = bf16[2048,384]{0,1:T(8,128)(2,1)} async-done(((bf16[256,384]{0,1:T(8,128)(2,1)}), bf16[2048,384]{0,1:T(8,128)(2,1)}) %all-gather.5.cloned.1.call-update) | async-done | bytes 1572880 | tf_op jit(solution)/shard_map/all_gather | solution.py:117
  61.5 112.0 %while.35 = (s32[]{:T(128)}, bf16[4,512,6,64]{1,3,2,0:T(8,128)(2,1)}, bf16[4,512,6]{1,2,0:T(8,128)(2,1)S(1)}, bf16[4,512,6]{1,2,0:T(8,128)(2,1)S(1)}, s32[4]{0:T...) while((s32[]{:T(128)}, ...), condition=%wide.region_5.6_spmd.clone, body=%wide.region_2.5_spmd.clone.sunk | while | flops 1060374528 | bytes 119003984 | solution.py:165
  80.9 7.9 fusion.78
  108.8 7.9 fusion.78
  136.9 7.9 fusion.78
  164.9 7.9 fusion.78
  178.6 31.7 %all_gather.23 = bf16[8,2048,6]{1,2,0:T(8,128)(2,1)S(1)} all-gather(bf16[1,2048,6]{1,2,0:T(8,128)(2,1)S(1)} %bitcast.154), channel_id=1, replica_groups=mesh['seq'=8,'tp'=4] {'seq'}, dimensions={0}, use_global_device_ids=true | all-gather | bytes 221184 | tf_op jit(solution)/shard_map/all_gather | solution.py:15
  211.8 32.3 %all_gather.24 = bf16[8,2048,6]{1,2,0:T(8,128)(2,1)S(1)} all-gather(bf16[1,2048,6]{1,2,0:T(8,128)(2,1)S(1)} %bitcast.155), channel_id=1, replica_groups=mesh['seq'=8,'tp'=4] {'seq'}, dimensions={0}, use_global_device_ids=true | all-gather | bytes 221184 | tf_op jit(solution)/shard_map/all_gather | solution.py:15
  244.4 112.8 %all-gather.7.cloned.1.call-done = bf16[8,2048,6,64]{1,3,2,0:T(8,128)(2,1)} async-done(((bf16[1,2048,6,64]{1,3,2,0:T(8,128)(2,1)}), bf16[8,2048,6,64]{1,3,2,0:T(8,128)(2,1)}) %all-gather.7.cloned.1.call-update) | async-done | bytes 12582928 | tf_op jit(solution)/shard_map/all_gather | solution.py:15
  360.7 6.6 copy.80
  367.3 147.2 %while.34 = (s32[]{:T(128)}, f32[2048,6,64]{2,1,0:T(8,128)}, f32[2048,6]{1,0:T(8,128)}, f32[2048,6]{1,0:T(8,128)S(1)}, bf16[8,2048,6]{1,2,0:T(8,128)(2,1)S(1)}, ...) while((s32[]{:T(128)}, f32[2048,6,64]{2,1,0:T(8,128)}, ...), condition=%wide.region_7.8_spmd, body=%wide.region_6.7_spmd.sunk | while | flops 3244037 | bytes 18334016 | solution.py:27
  374.3 4.2 copy.103
  378.6 9.7 fusion.73
  395.3 4.2 copy.103
  399.6 9.7 fusion.73
  416.4 4.2 copy.103
  420.6 9.7 fusion.73
  437.4 4.2 copy.103
  441.7 9.7 fusion.73
  458.4 4.2 copy.103
  462.7 9.7 fusion.73
  479.5 4.2 copy.103
  483.7 9.7 fusion.73
  500.5 4.2 copy.103
  504.8 9.7 fusion.73
  514.5 6.3 copy.86
  524.8 31.7 %all-reduce.3.cloned.1.call-done = bf16[256,1536]{1,0:T(8,128)(2,1)} async-done(((bf16[256,1536]{1,0:T(8,128)(2,1)}), bf16[256,1536]{1,0:T(8,128)(2,1)}) %all-reduce.3.cloned.1.call-update) | async-done | bytes 786448 | tf_op jit(solution)/shard_map/psum | solution.py:177
  560.0 596.4 %all-gather.9.cloned.1.call-done = bf16[10,2,1536,512]{3,2,1,0:T(8,128)(2,1)} async-done(((bf16[10,2,192,512]{3,2,1,0:T(8,128)(2,1)}), bf16[10,2,1536,512]{3,2,1,0:T(8,128)(2,1)}) %all-gather.9.cloned.1.call-update) | async-done | bytes 31457296 | tf_op jit(solution)/shard_map/all_gather | solution.py:192
  1156.3 17.0 %fusion.36 = f32[256,10,2,512]{3,0,2,1:T(8,128)} fusion(bf16[10,2,1536,512]{3,2,1,0:T(8,128)(2,1)} %all-gather.9.cloned.1.call-done, bf16[256,1536]{1,0:T(8,128)(2,1)S(1)} %multiply_convert_fusion), kind=kOutput, calls=%fused_computation.67 | convolution fusion | flops 8053063680 | bytes 42729472 | tf_op jit(solution)/shard_map/td,ecdf->tecf/dot_general | solution.py:189
  1173.3 199.8 %all-gather.11.cloned.1.call-done = bf16[10,512,1536]{2,1,0:T(8,128)(2,1)} async-done(((bf16[10,64,1536]{2,1,0:T(8,128)(2,1)}), bf16[10,512,1536]{2,1,0:T(8,128)(2,1)}) %all-gather.11.cloned.1.call-update) | async-done | bytes 15728656 | tf_op jit(solution)/shard_map/all_gather | solution.py:199
  1373.2 13.9 fusion.29
  1387.1 33.0 %all-reduce.5.cloned.1.call-done = bf16[256,1536]{1,0:T(8,128)(2,1)} async-done(((bf16[256,1536]{1,0:T(8,128)(2,1)}), bf16[256,1536]{1,0:T(8,128)(2,1)}) %all-reduce.5.cloned.1.call-update) | async-done | bytes 786448 | tf_op jit(solution)/shard_map/psum | solution.py:202
  (282 shorter events, 147.8 us)
Async XLA Ops:
  7.2 514.8 %copy-start = (bf16[384,1536]{1,0:T(8,128)(2,1)S(1)}, bf16[384,1536]{1,0:T(8,128)(2,1)}, u32[]{:S(2)}) copy-start(bf16[384,1536]{1,0:T(8,128)(2,1)} %param.26) | copy-start | bytes 3538948
  7.2 54.3 %copy-start.14 = (s32[4]{0:T(128)S(1)}, s32[4]{0:T(128)}, u32[]{:S(2)}) copy-start(s32[4]{0:T(128)} %param.25) | copy-start | bytes 52
  7.2 54.3 %all-gather.5.cloned.1.call-start = ((), (), s32[]{:S(2)}) async-start(), calls=%async_computation | async-start | bytes 1769472 | tf_op jit(solution)/shard_map/all_gather | solution.py:117
  13.4 343.9 %all-gather.7.cloned.1.call-start = ((), (), s32[]{:S(2)}) async-start(), calls=%async_computation.1 | async-start | bytes 14155776 | tf_op jit(solution)/shard_map/all_gather | solution.py:15
  178.6 377.9 %all-reduce.3.cloned.1.call-start = ((), (), s32[]{:S(2)}) async-start(), calls=%async_computation.2 | async-start | bytes 1572864 | tf_op jit(solution)/shard_map/psum | solution.py:177
  378.6 9.7 copy-start.3
  378.6 9.7 copy-start.8
  378.6 9.7 copy-start.10
  399.6 9.7 copy-start.3
  399.6 9.7 copy-start.8
  399.6 9.7 copy-start.10
  420.6 9.7 copy-start.3
  420.6 9.7 copy-start.8
  420.6 9.7 copy-start.10
  441.7 9.7 copy-start.3
  441.7 9.7 copy-start.8
  441.7 9.7 copy-start.10
  462.7 9.7 copy-start.3
  462.7 9.7 copy-start.8
  462.7 9.7 copy-start.10
  483.7 9.7 copy-start.3
  483.7 9.7 copy-start.8
  483.7 9.7 copy-start.10
  504.8 9.7 copy-start.8
  504.8 9.7 copy-start.10
  520.8 35.7 %copy-start.5 = (bf16[256,1536]{1,0:T(8,128)(2,1)S(1)}, bf16[256,1536]{1,0:T(8,128)(2,1)}, u32[]{:S(2)}) copy-start(bf16[256,1536]{1,0:T(8,128)(2,1)} %param.18) | copy-start | bytes 2359300
  523.5 35.9 %copy-start.11 = (bf16[1536,40]{0,1:T(8,128)(2,1)S(1)}, bf16[1536,40]{0,1:T(8,128)(2,1)}, u32[]{:S(2)}) copy-start(bf16[1536,40]{0,1:T(8,128)(2,1)} %param.28) | copy-start | bytes 368644
  523.5 36.3 %copy-start.12 = (s32[256,8]{0,1:T(8,128)S(1)}, s32[256,8]{0,1:T(8,128)}, u32[]{:S(2)}) copy-start(s32[256,8]{0,1:T(8,128)} %param.29) | copy-start | bytes 24580
  523.5 632.8 %all-gather.9.cloned.1.call-start = ((), (), s32[]{:S(2)}) async-start(), calls=%async_computation.3 | async-start | bytes 35389440 | tf_op jit(solution)/shard_map/all_gather | solution.py:192
  524.1 849.1 %all-gather.11.cloned.1.call-start = ((), (), s32[]{:S(2)}) async-start(), calls=%async_computation.4 | async-start | bytes 17694720 | tf_op jit(solution)/shard_map/all_gather | solution.py:199
  524.7 895.4 %all-reduce.5.cloned.1.call-start = ((), (), s32[]{:S(2)}) async-start(), calls=%async_computation.5 | async-start | bytes 1572864 | tf_op jit(solution)/shard_map/psum | solution.py:202
  1173.3 246.8 %copy-start.6 = (bf16[256,1536]{1,0:T(8,128)(2,1)S(1)}, bf16[256,1536]{1,0:T(8,128)(2,1)}, u32[]{:S(2)}) copy-start(bf16[256,1536]{1,0:T(8,128)(2,1)} %all-reduce.3.cloned.1.call-done) | copy-start | bytes 2359300
  (29 other events, 70.7 us)
Sparse Core Ops, SparseCore 0:
  13.5 47.9 all-gather.4
  178.7 178.4 all-gather.6
  523.6 32.8 all-reduce.2
  557.9 598.4 all-gather.8
  1158.4 214.7 all-gather.10
  1387.2 32.7 all-reduce.4
where the time goes:
time: 1430 us
  waiting for transfers between devices  1020 us (71%)
  other arithmetic  129 us (9%)
  local copies, waits for them, and re-layouts  112 us (8%)
  matrix products  78.9 us (6%)
  blocking collectives  64 us (4%)
  between operations  14.4 us (1%)
    all_gather x1, waiting for transfers between devices, per_device(): lax.all_gather(w_gate_up, 'seq', axis=2, tiled=True)  596 us
    all_gather x1, waiting for transfers between devices, per_device(): lax.all_gather(w_down, 'seq', axis=1, tiled=True)  200 us
    all_gather x1, waiting for transfers between devices, combined_all(): lax.all_gather(a.astype(kind), axis)  113 us
    add x7, other arithmetic, join_parts(): out_a * factor_a[..., None] + out_b * factor_b[..., None]  67.9 us
    all_gather x2, blocking collectives, combined_all(): lax.all_gather(a.astype(kind), axis)  64 us
    all_gather x1, waiting for transfers between devices, per_device(): lax.all_gather(query_vector.reshape(tok_rows, local_q * HEAD_SIZE), 'seq'...  45.8 us
    dynamic_slice x35, local copies, waits for them, and re-layouts, take(): lax.dynamic_index_in_dim(a, source, 0, False).astype(own.dtype)  44.7 us
    psum x1, waiting for transfers between devices, per_device(): expert_out = lax.psum(moe_part.astype(jnp.bfloat16), 'tp')  33 us
  transfers between devices with their start and end apart: 6, of which 6 were waited for; matrix products, arithmetic and copies ran while one was open for 2% of the time, Pallas kernels for 0%

commit v1 on v0

--- a/solution.py
+++ b/solution.py
@@ -8,6 +8,24 @@
 EPS = 1e-05
 THETA = 10000.0
 NEGATIVE = -1e30
+
+
+def gather_around(array, axis, dim):
+    ways, here, step = (lax.axis_size(axis), lax.axis_index(axis), array.shape[dim])
+    shape = [n * ways if d == dim else n for d, n in enumerate(array.shape)]
+    full = lax.dynamic_update_slice_in_dim(
+        jnp.zeros(shape, array.dtype), array, here * step, axis=dim
+    )
+    going_up = going_down = array
+    for far in range(1, ways // 2 + 1):
+        going_up = lax.ppermute(going_up, axis, [(d, (d + 1) % ways) for d in range(ways)])
+        full = lax.dynamic_update_slice_in_dim(full, going_up, (here - far) % ways * step, axis=dim)
+        if 2 * far < ways:
+            going_down = lax.ppermute(going_down, axis, [(d, (d - 1) % ways) for d in range(ways)])
+            full = lax.dynamic_update_slice_in_dim(
+                full, going_down, (here + far) % ways * step, axis=dim
+            )
+    return full
 
 
 def combined_all(x, axis, join):
@@ -194,10 +212,7 @@
     )
     hidden = (jax.nn.silu(both[:, :, 0]) * both[:, :, 1] * share[:, :, None]).astype(jnp.bfloat16)
     moe_part = jnp.einsum(
-        "tef,efd->td",
-        hidden,
-        lax.all_gather(w_down, "seq", axis=1, tiled=True),
-        preferred_element_type=jnp.float32,
+        "tef,efd->td", hidden, gather_around(w_down, "seq", 1), preferred_element_type=jnp.float32
     )
     expert_out = lax.psum(moe_part.astype(jnp.bfloat16), "tp")
     return (attn_out, expert_out)

time: 1430 us -> 1490 us (1.042)
  waiting for transfers between devices: 1020 us -> 1040 us
  matrix products: 78.9 us -> 96.3 us
  local copies, waits for them, and re-layouts: 112 us -> 128 us
    ppermute x0 -> x7, waiting for transfers between devices: none -> 609 us  [the longest x4 357 us: gather_around(): lax.ppermute(going_up, axis, [(d, (d + 1) % ways) for d in range(ways)])]
    all_gather x1, waiting for transfers between devices: 596 us -> 236 us  [per_device(): lax.all_gather(w_gate_up, 'seq', axis=2, tiled=True)]
    all_gather x1 -> x0, waiting for transfers between devices: 200 us -> none  [per_device(): lax.all_gather(w_down, 'seq', axis=1, tiled=True)]
    psum x1, waiting for transfers between devices: 31.7 us -> 0.01 us  [per_device(): attn = lax.psum(attn_part.astype(jnp.bfloat16), 'tp').astype(jnp.float32)]
    dynamic_update_slice x0 -> x8, local copies, waits for them, and re-layouts: none -> 19.5 us  [the longest x4 10.5 us: gather_around(): lax.dynamic_update_slice_in_dim(full, going_up, (here - far) % ways * ste...]
    dot_general x4, matrix products: 10.5 us -> 27.7 us  [one_request(): jnp.einsum('nhgd,khd->hgnk', query_rows, keys, preferred_element_type=jnp...]
  transfers between devices with their start and end apart: 6 -> 12, of which waited for: 6 -> 9; matrix products, arithmetic and copies ran while one was open for 2% -> 2% of each run, Pallas kernels for 0% -> 0%
where the time goes in v1:
time: 1490 us
  waiting for transfers between devices  1040 us (70%)
  local copies, waits for them, and re-layouts  128 us (9%)
  other arithmetic  121 us (8%)
  matrix products  96.3 us (6%)
  blocking collectives  64 us (4%)
    ppermute x4, waiting for transfers between devices, gather_around(): lax.ppermute(going_up, axis, [(d, (d + 1) % ways) for d in range(ways)])  357 us
    ppermute x3, waiting for transfers between devices, gather_around(): lax.ppermute(going_down, axis, [(d, (d - 1) % ways) for d in range(ways)])  252 us
    all_gather x1, waiting for transfers between devices, per_device(): lax.all_gather(w_gate_up, 'seq', axis=2, tiled=True)  236 us
    all_gather x1, waiting for transfers between devices, combined_all(): lax.all_gather(a.astype(kind), axis)  112 us
    all_gather x2, blocking collectives, combined_all(): lax.all_gather(a.astype(kind), axis)  64 us
    add x7, other arithmetic, join_parts(): out_a * factor_a[..., None] + out_b * factor_b[..., None]  58.5 us
    all_gather x1, waiting for transfers between devices, per_device(): lax.all_gather(query_vector.reshape(tok_rows, local_q * HEAD_SIZE), 'seq'...  45.8 us
    dynamic_slice x35, local copies, waits for them, and re-layouts, take(): lax.dynamic_index_in_dim(a, source, 0, False).astype(own.dtype)  45 us
  transfers between devices with their start and end apart: 12, of which 9 were waited for; matrix products, arithmetic and copies ran while one was open for 2% of the time, Pallas kernels for 0%

profile of v1, /device:TPU:0, one launch (start us, length us, event | category | flops | bytes accessed | tf_op | source)
XLA Modules:
  0.0 1487.4 jit_solution(11154716383032577080)
XLA Ops:
  15.7 45.8 %all-gather.4.cloned.1.call-done = bf16[2048,384]{0,1:T(8,128)(2,1)} async-done(((bf16[256,384]{0,1:T(8,128)(2,1)}), bf16[2048,384]{0,1:T(8,128)(2,1)}) %all-gather.4.cloned.1.call-update) | async-done | bytes 1572880 | tf_op jit(solution)/shard_map/all_gather | solution.py:135
  61.5 128.7 %while.35 = (s32[]{:T(128)}, bf16[4,512,6,64]{1,3,2,0:T(8,128)(2,1)}, bf16[4,512,6]{1,2,0:T(8,128)(2,1)S(1)}, bf16[4,512,6]{1,2,0:T(8,128)(2,1)S(1)}, s32[4]{0:T...) while((s32[]{:T(128)}, ...), condition=%wide.region_5.6_spmd.clone, body=%wide.region_2.5_spmd.clone.sunk | while | flops 1060374528 | bytes 103274912 | solution.py:183
  71.0 6.9 fusion.77
  79.7 8.0 fusion.78
  103.2 6.9 fusion.77
  111.8 8.0 fusion.78
  135.4 6.9 fusion.77
  144.0 8.0 fusion.78
  167.5 6.9 fusion.77
  176.2 8.0 fusion.78
  195.4 31.7 %all_gather.20 = bf16[8,2048,6]{1,2,0:T(8,128)(2,1)S(1)} all-gather(bf16[1,2048,6]{1,2,0:T(8,128)(2,1)S(1)} %bitcast.156), channel_id=1, replica_groups=mesh['seq'=8,'tp'=4] {'seq'}, dimensions={0}, use_global_device_ids=true | all-gather | bytes 221184 | tf_op jit(solution)/shard_map/all_gather | solution.py:33
  228.5 32.3 %all_gather.21 = bf16[8,2048,6]{1,2,0:T(8,128)(2,1)S(1)} all-gather(bf16[1,2048,6]{1,2,0:T(8,128)(2,1)S(1)} %bitcast.157), channel_id=1, replica_groups=mesh['seq'=8,'tp'=4] {'seq'}, dimensions={0}, use_global_device_ids=true | all-gather | bytes 221184 | tf_op jit(solution)/shard_map/all_gather | solution.py:33
  262.1 111.8 %all-gather.6.cloned.1.call-done = bf16[8,2048,6,64]{1,3,2,0:T(8,128)(2,1)} async-done(((bf16[1,2048,6,64]{1,3,2,0:T(8,128)(2,1)}), bf16[8,2048,6,64]{1,3,2,0:T(8,128)(2,1)}) %all-gather.6.cloned.1.call-update) | async-done | bytes 12582928 | tf_op jit(solution)/shard_map/all_gather | solution.py:33
  377.4 6.6 copy.80
  384.0 128.1 %while.34 = (s32[]{:T(128)}, f32[2048,6,64]{2,1,0:T(8,128)}, f32[2048,6]{1,0:T(8,128)}, f32[2048,6]{1,0:T(8,128)}, bf16[8,2048,6]{1,2,0:T(8,128)(2,1)S(1)}, /*in...) while((s32[]{:T(128)}, f32[2048,6,64]{2,1,0:T(8,128)}, ...), condition=%wide.region_7.8_spmd, body=%wide.region_6.7_spmd.sunk | while | flops 3244037 | bytes 21086388 | solution.py:45
  394.0 8.4 fusion.73
  412.3 8.4 fusion.73
  430.5 8.4 fusion.73
  448.8 8.4 fusion.73
  467.1 8.4 fusion.73
  485.4 8.4 fusion.73
  503.7 8.4 fusion.73
  527.5 195.9 %collective-permute-done = bf16[10,64,1536]{2,1,0:T(8,128)(2,1)S(1)} collective-permute-done((bf16[10,64,1536]{2,1,0:T(8,128)(2,1)S(1)}, bf16[10,64,1536]{2,1,0:T(8,128)(2,1)S(1)}, u32[]{:S(2)}, u32[]{:S(2)}) %collective-permute-start) | collective-permute-done | bytes 1966112 | tf_op jit(solution)/shard_map/ppermute | solution.py:21
  725.9 83.1 %collective-permute-done.1 = bf16[10,64,1536]{2,1,0:T(8,128)(2,1)S(1)} collective-permute-done((bf16[10,64,1536]{2,1,0:T(8,128)(2,1)S(1)}, bf16[10,64,1536]{2,1,0:T(8,128)(2,1)S(1)}, u32[]{:S(2)}, u32[]{:S(2)}) %collective-permute-start.1) | collective-permute-done | bytes 1966112 | tf_op jit(solution)/shard_map/ppermute | solution.py:24
  811.1 169.1 %collective-permute-done.3 = bf16[10,64,1536]{2,1,0:T(8,128)(2,1)} collective-permute-done((bf16[10,64,1536]{2,1,0:T(8,128)(2,1)S(1)}, bf16[10,64,1536]{2,1,0:T(8,128)(2,1)}, u32[]{:S(2)}, u32[]{:S(2)}) %collective-permute-start.3) | collective-permute-done | bytes 1966112 | tf_op jit(solution)/shard_map/ppermute | solution.py:24
  980.5 92.4 %collective-permute-done.4 = bf16[10,64,1536]{2,1,0:T(8,128)(2,1)} collective-permute-done((bf16[10,64,1536]{2,1,0:T(8,128)(2,1)}, bf16[10,64,1536]{2,1,0:T(8,128)(2,1)}, u32[]{:S(2)}, u32[]{:S(2)}) %collective-permute-start.4) | collective-permute-done | bytes 1966112 | tf_op jit(solution)/shard_map/ppermute | solution.py:21
  1075.4 6.9 broadcast_in_dim.115
  1099.5 68.9 %collective-permute-done.6 = bf16[10,64,1536]{2,1,0:T(8,128)(2,1)} collective-permute-done((bf16[10,64,1536]{2,1,0:T(8,128)(2,1)}, bf16[10,64,1536]{2,1,0:T(8,128)(2,1)}, u32[]{:S(2)}, u32[]{:S(2)}) %collective-permute-start.6) | collective-permute-done | bytes 1966112 | tf_op jit(solution)/shard_map/ppermute | solution.py:21
  1174.9 235.5 %all-gather.8.cloned.1.call-done = bf16[10,2,1536,512]{3,2,1,0:T(8,128)(2,1)} async-done(((bf16[10,2,192,512]{3,2,1,0:T(8,128)(2,1)}), bf16[10,2,1536,512]{3,2,1,0:T(8,128)(2,1)}) %all-gather.8.cloned.1.call-update) | async-done | bytes 31457296 | tf_op jit(solution)/shard_map/all_gather | solution.py:210
  1410.4 16.5 %fusion.36 = f32[256,10,2,512]{3,0,2,1:T(8,128)} fusion(bf16[10,2,1536,512]{3,2,1,0:T(8,128)(2,1)} %all-gather.8.cloned.1.call-done, bf16[256,1536]{1,0:T(8,128)(2,1)S(1)} %multiply_convert_fusion), kind=kOutput, calls=%fused_computation.67 | convolution fusion | flops 8053063680 | bytes 42729472 | tf_op jit(solution)/shard_map/td,ecdf->tecf/dot_general | solution.py:207
  1427.0 14.0 fusion.29
  1441.0 37.0 %all-reduce.5.cloned.1.call-done = bf16[256,1536]{1,0:T(8,128)(2,1)} async-done(((bf16[256,1536]{1,0:T(8,128)(2,1)}), bf16[256,1536]{1,0:T(8,128)(2,1)}) %all-reduce.5.cloned.1.call-update) | async-done | bytes 786448 | tf_op jit(solution)/shard_map/psum | solution.py:217
  (270 shorter events, 196.6 us)
Async XLA Ops:
  7.2 513.4 %copy-start = (bf16[384,1536]{1,0:T(8,128)(2,1)S(1)}, bf16[384,1536]{1,0:T(8,128)(2,1)}, u32[]{:S(2)}) copy-start(bf16[384,1536]{1,0:T(8,128)(2,1)} %param.26) | copy-start | bytes 3538948
  7.2 54.3 %copy-start.13 = (s32[4]{0:T(128)S(1)}, s32[4]{0:T(128)}, u32[]{:S(2)}) copy-start(s32[4]{0:T(128)} %param.25) | copy-start | bytes 52
  7.2 54.3 %all-gather.4.cloned.1.call-start = ((), (), s32[]{:S(2)}) async-start(), calls=%async_computation | async-start | bytes 1769472 | tf_op jit(solution)/shard_map/all_gather | solution.py:135
  13.4 360.6 %all-gather.6.cloned.1.call-start = ((), (), s32[]{:S(2)}) async-start(), calls=%async_computation.1 | async-start | bytes 14155776 | tf_op jit(solution)/shard_map/all_gather | solution.py:33
  79.6 8.9 slice-start
  79.7 9.2 slice-start.2
  79.7 10.1 slice-start.3
  111.8 9.2 slice-start.2
  111.8 10.1 slice-start.3
  144.0 8.9 slice-start
  144.0 8.9 slice-start.1
  144.0 9.1 slice-start.2
  144.0 10.1 slice-start.3
  176.2 8.9 slice-start
  176.2 9.2 slice-start.2
  176.2 10.1 slice-start.3
  195.3 976.1 %all-reduce.3.cloned.1.call-start = ((), (), s32[]{:S(2)}) async-start(), calls=%async_computation.2 | async-start | bytes 1572864 | tf_op jit(solution)/shard_map/psum | solution.py:195
  518.4 462.1 %copy-start.12 = (bf16[1536]{0:T(1024)(128)(2,1)S(1)}, bf16[1536]{0:T(1024)(128)(2,1)}, u32[]{:S(2)}) copy-start(bf16[1536]{0:T(1024)(128)(2,1)} %param.27) | copy-start | bytes 9220
  522.1 888.4 %all-gather.8.cloned.1.call-start = ((), (), s32[]{:S(2)}) async-start(), calls=%async_computation.3 | async-start | bytes 35389440 | tf_op jit(solution)/shard_map/all_gather | solution.py:210
  522.6 955.3 %all-reduce.5.cloned.1.call-start = ((), (), s32[]{:S(2)}) async-start(), calls=%async_computation.4 | async-start | bytes 1572864 | tf_op jit(solution)/shard_map/psum | solution.py:217
  522.7 200.7 %collective-permute-start = (bf16[10,64,1536]{2,1,0:T(8,128)(2,1)S(1)}, bf16[10,64,1536]{2,1,0:T(8,128)(2,1)S(1)}, u32[]{:S(2)}, u32[]{:S(2)}) collective-permute-start(bf16[10,64,1536]{2,1,0:T(8,128)(2,1)S(1)} %copy-done.5), channel_id=1, source_target_pairs={{0,4},{4,8},{8,12},{12,16},{16,20},{20,24},{24,28},{28,0},{1,5},{5... | collective-permute-start | bytes 5898248 | tf_op jit(solution)/shard_map/ppermute | solution.py:21
  523.3 285.7 %collective-permute-start.1 = (bf16[10,64,1536]{2,1,0:T(8,128)(2,1)S(1)}, bf16[10,64,1536]{2,1,0:T(8,128)(2,1)S(1)}, u32[]{:S(2)}, u32[]{:S(2)}) collective-permute-start(bf16[10,64,1536]{2,1,0:T(8,128)(2,1)S(1)} %copy-done.5), channel_id=1, source_target_pairs={{0,28},{4,0},{8,4},{12,8},{16,12},{20,16},{24,20},{28,24},{1,29},{... | collective-permute-start | bytes 5898248 | tf_op jit(solution)/shard_map/ppermute | solution.py:24
  723.4 85.6 %copy-start.6 = (bf16[10,64,1536]{2,1,0:T(8,128)(2,1)}, bf16[10,64,1536]{2,1,0:T(8,128)(2,1)S(1)}, u32[]{:S(2)}) copy-start(bf16[10,64,1536]{2,1,0:T(8,128)(2,1)S(1)} %collective-permute-done) | copy-start | bytes 5898244
  723.4 87.7 %collective-permute-start.2 = (bf16[10,64,1536]{2,1,0:T(8,128)(2,1)S(1)}, bf16[10,64,1536]{2,1,0:T(8,128)(2,1)}, u32[]{:S(2)}, u32[]{:S(2)}) collective-permute-start(bf16[10,64,1536]{2,1,0:T(8,128)(2,1)S(1)} %collective-permute-done), channel_id=1, source_target_pairs={{0,4},{4,8},{8,12},{12,16},{16,20},{20,24},{24,28},{28,0},{1,5},{5... | collective-permute-start | bytes 5898248 | tf_op jit(solution)/shard_map/ppermute | solution.py:21
  809.0 171.1 %collective-permute-start.3 = (bf16[10,64,1536]{2,1,0:T(8,128)(2,1)S(1)}, bf16[10,64,1536]{2,1,0:T(8,128)(2,1)}, u32[]{:S(2)}, u32[]{:S(2)}) collective-permute-start(bf16[10,64,1536]{2,1,0:T(8,128)(2,1)S(1)} %collective-permute-done.1), channel_id=1, source_target_pairs={{0,28},{4,0},{8,4},{12,8},{16,12},{20,16},{24,20},{28,24},{1,29},{... | collective-permute-start | bytes 5898248 | tf_op jit(solution)/shard_map/ppermute | solution.py:24
  811.1 261.8 %collective-permute-start.4 = (bf16[10,64,1536]{2,1,0:T(8,128)(2,1)}, bf16[10,64,1536]{2,1,0:T(8,128)(2,1)}, u32[]{:S(2)}, u32[]{:S(2)}) collective-permute-start(bf16[10,64,1536]{2,1,0:T(8,128)(2,1)} %collective-permute-done.2), channel_id=1, source_target_pairs={{0,4},{4,8},{8,12},{12,16},{16,20},{20,24},{24,28},{28,0},{1,5},{5... | collective-permute-start | bytes 5898248 | tf_op jit(solution)/shard_map/ppermute | solution.py:21
  980.1 116.4 %collective-permute-start.5 = (bf16[10,64,1536]{2,1,0:T(8,128)(2,1)}, bf16[10,64,1536]{2,1,0:T(8,128)(2,1)}, u32[]{:S(2)}, u32[]{:S(2)}) collective-permute-start(bf16[10,64,1536]{2,1,0:T(8,128)(2,1)} %collective-permute-done.3), channel_id=1, source_target_pairs={{0,28},{4,0},{8,4},{12,8},{16,12},{20,16},{24,20},{28,24},{1,29},{... | collective-permute-start | bytes 5898248 | tf_op jit(solution)/shard_map/ppermute | solution.py:24
  1072.9 95.5 %collective-permute-start.6 = (bf16[10,64,1536]{2,1,0:T(8,128)(2,1)}, bf16[10,64,1536]{2,1,0:T(8,128)(2,1)}, u32[]{:S(2)}, u32[]{:S(2)}) collective-permute-start(bf16[10,64,1536]{2,1,0:T(8,128)(2,1)} %collective-permute-done.4), channel_id=1, source_target_pairs={{0,4},{4,8},{8,12},{12,16},{16,20},{20,24},{24,28},{28,0},{1,5},{5... | collective-permute-start | bytes 5898248 | tf_op jit(solution)/shard_map/ppermute | solution.py:21
  1093.5 77.9 %copy-start.3 = (bf16[256,1536]{1,0:T(8,128)(2,1)S(1)}, bf16[256,1536]{1,0:T(8,128)(2,1)}, u32[]{:S(2)}) copy-start(bf16[256,1536]{1,0:T(8,128)(2,1)} %param.18) | copy-start | bytes 2359300
  1096.5 77.8 %copy-start.10 = (bf16[1536,40]{0,1:T(8,128)(2,1)S(1)}, bf16[1536,40]{0,1:T(8,128)(2,1)}, u32[]{:S(2)}) copy-start(bf16[1536,40]{0,1:T(8,128)(2,1)} %param.28) | copy-start | bytes 368644
  1099.5 75.1 %copy-start.11 = (s32[256,8]{0,1:T(8,128)S(1)}, s32[256,8]{0,1:T(8,128)}, u32[]{:S(2)}) copy-start(s32[256,8]{0,1:T(8,128)} %param.29) | copy-start | bytes 24580
  1427.0 51.0 %copy-start.4 = (bf16[256,1536]{1,0:T(8,128)(2,1)S(1)}, bf16[256,1536]{1,0:T(8,128)(2,1)}, u32[]{:S(2)}) copy-start(bf16[256,1536]{1,0:T(8,128)(2,1)} %all-reduce.3.cloned.1.call-done) | copy-start | bytes 2359300
  (17 other events, 88.3 us)
Sparse Core Ops, SparseCore 0:
  13.5 47.9 all-gather.3
  195.4 178.4 all-gather.5
  522.2 32.8 all-reduce.2
  556.4 853.9 all-gather.7
  1441.1 36.8 all-reduce.4
